TPU v7x, 256 devices: a whole 4x4x8 slice. The times are simulated.
256 devices in a mesh: seq: 16 (over x, y), fsdp: 16 (over z, core).
Axes of the slice: x: 4, y: 4, z: 8, core: 2. Of those that a mesh axis runs over, the one named last changes fastest.
Arguments:
- patches: bfloat16 [16, 8704, 1176], P('fsdp', 'seq'), may hold values from -6 to 6
- send_slot: int32 [16, 272], P('fsdp', 'seq'), may hold values from 0 to 271, as said below
- segments: int32 [16, 272], P('fsdp'), may hold values from 0 to 33, never falling along the last dimension, each value on 1 to 24 neighbouring positions
- stem_weight: bfloat16 [3584, 1176], P('fsdp'), may hold values from -0.1875 to 0.1875
- norm_gain: bfloat16 [3584], P('fsdp'), may hold values from 0.099609375 to 1.8984375
- conv_kernel: bfloat16 [5, 3584], P(None, 'fsdp'), may hold values from -3 to 3
- cotangent: bfloat16 [16, 8704, 3584], P('fsdp', 'seq'), may hold values from -6 to 6
Outputs:
- features: bfloat16 [16, 8704, 3584], P('fsdp', 'seq')
- grad_patches: bfloat16 [16, 8704, 1176], P('fsdp', 'seq')
- grad_weight: bfloat16 [3584, 1176], P('fsdp')
- grad_channels: float32 [6, 3584], P(None, 'fsdp')
Inputs may be any that keep to these rules, and one draw needn't show every extreme that they name: `send_slot`: each row is a permutation of the packed slots. At most 2 frame slots of one device go to one device's packed slots, and every device sends exactly 2 to some device; within a row the number that device s sends to device (s + o) modulo the seq axis size depends on o alone. `segments`: ids never fall along a row; a clip holds 1 to 24 slots, one exactly 24.
All inputs are finite; a program needn't handle non-finite values.
Results may differ from a plain program's by a relative error of at most 0.0056.
Values may be sent and summed in bfloat16 or wider, within the bound.
A program may use at most 192 MiB of HBM per device.

v0:
```python
import math
import jax
import jax.numpy as jnp
from jax import lax
from jax.sharding import PartitionSpec as P

EPSILON = 1e-06


def extended_2(cells, sides, width):
    for axis, dim in sides:
        count = lax.axis_size(axis)
        ends = count - 1
        head = lax.slice_in_dim(cells, 0, width, axis=dim)
        tail = lax.slice_in_dim(cells, cells.shape[dim] - width, cells.shape[dim], axis=dim)
        cells = jnp.concatenate(
            [
                lax.ppermute(tail, axis, [(i, (i + 1) % count) for i in range(ends)]),
                cells,
                lax.ppermute(head, axis, [((i + 1) % count, i) for i in range(ends)]),
            ],
            axis=dim,
        )
    return cells


def slot_mask(segment_row, centre):
    slot_total = segment_row.shape[0]
    safe_centre = jnp.clip(centre, 0, slot_total - 1)
    columns = []
    for offset in range(5):
        neighbour = centre + (offset - 2)
        inside = (neighbour >= 0) & (neighbour < slot_total) & (centre >= 0) & (centre < slot_total)
        same_clip = segment_row[jnp.clip(neighbour, 0, slot_total - 1)] == segment_row[safe_centre]
        columns.append((inside & same_clip).astype(jnp.float32))
    return jnp.stack(columns, axis=1)


def temporal_mix(padded, clip_mask, kernel, slot_total):
    kernel_wide = kernel.astype(jnp.float32)
    result = padded[0:slot_total].astype(jnp.float32) * (
        clip_mask[:, 0][:, None, None] * kernel_wide[0][None, None, :]
    )
    for offset in range(1, 5):
        addend = padded[offset : offset + slot_total].astype(jnp.float32) * (
            clip_mask[:, offset][:, None, None] * kernel_wide[offset][None, None, :]
        )
        result = result + addend
    return result


def temporal_back(slope_padded, mask_padded, kernel, slot_total):
    kernel_wide = kernel.astype(jnp.float32)
    result = jnp.zeros((slot_total,) + slope_padded.shape[1:], jnp.float32)
    for offset in range(5):
        first_row = 4 - offset
        weights_row = (
            mask_padded[first_row : first_row + slot_total, offset][:, None, None]
            * kernel_wide[offset][None, None, :]
        )
        result = (
            result
            + slope_padded[first_row : first_row + slot_total].astype(jnp.float32) * weights_row
        )
    return result


def kernel_sums(slope_blocks, padded, clip_mask, slot_total):
    stacked = []
    for offset in range(5):
        product = jnp.sum(
            slope_blocks.astype(jnp.float32)
            * padded[offset : offset + slot_total].astype(jnp.float32),
            axis=1,
        )
        stacked.append(jnp.sum(product * clip_mask[:, offset][:, None], axis=0))
    return jnp.stack(stacked, axis=0)


def rim_rows(values, margin):
    return extended_2(values, (("seq", 0),), margin)


def shards(patches, send_slot, segments, stem_weight, norm_gain, conv_kernel, cotangent):
    seq_size = lax.axis_size("seq")
    fsdp_size = lax.axis_size("fsdp")
    seq_index = lax.axis_index("seq")
    slot_count = send_slot.shape[1]
    tokens = patches.shape[1]
    slot_rows = tokens // slot_count
    pixel_width = patches.shape[2]
    capacity = 2 * slot_count // seq_size
    destination = send_slot[0]
    owner_index = destination // slot_count
    same_owner = owner_index[:, None] == owner_index[None, :]
    earlier = destination[None, :] < destination[:, None]
    ranking = jnp.sum((same_owner & earlier).astype(jnp.int32), axis=1)
    buffer_row = owner_index * capacity + ranking
    frames = patches[0].reshape(slot_count, slot_rows, pixel_width)
    outbox = (
        jnp.zeros((seq_size * capacity, slot_rows, pixel_width), jnp.bfloat16)
        .at[buffer_row]
        .set(frames)
    )
    position = (
        jnp.full((seq_size * capacity,), -1.0, jnp.float32)
        .at[buffer_row]
        .set((destination % slot_count).astype(jnp.float32))
        .astype(jnp.bfloat16)
    )
    incoming, arrived = (
        lax.all_to_all(outbox, "seq", split_axis=0, concat_axis=0, tiled=True),
        lax.all_to_all(position, "seq", split_axis=0, concat_axis=0, tiled=True),
    )
    arrived_float = arrived.astype(jnp.float32)
    target = jnp.where(arrived_float >= 0.0, arrived_float, float(slot_count)).astype(jnp.int32)
    packed = (
        jnp.zeros((slot_count + 1, slot_rows, pixel_width), jnp.bfloat16)
        .at[target]
        .set(incoming)[:slot_count]
        .reshape(tokens, pixel_width)
    )
    weight_full, gain_low, kernel_full = (
        lax.all_gather(stem_weight, "fsdp", axis=0, tiled=True),
        lax.all_gather(norm_gain, "fsdp", axis=0, tiled=True),
        lax.all_gather(conv_kernel, "fsdp", axis=1, tiled=True),
    )
    gain_wide = gain_low.astype(jnp.float32)
    channels = weight_full.shape[0]
    stem_out = lax.dot_general(
        packed, weight_full, (((1,), (1,)), ((), ())), preferred_element_type=jnp.float32
    )
    inv_rms = lax.rsqrt(jnp.mean(stem_out * stem_out, axis=1, keepdims=True) + EPSILON)
    unit_rows = stem_out * inv_rms
    normed = (unit_rows * gain_wide).astype(jnp.bfloat16)
    segment_row = segments[0]
    centre = seq_index * slot_count + jnp.arange(slot_count, dtype=jnp.int32)
    extended = seq_index * slot_count + jnp.arange(-2, slot_count + 2, dtype=jnp.int32)
    clip_mask = slot_mask(segment_row, centre)
    mask_padded = slot_mask(segment_row, extended)
    padded = rim_rows(normed, 2 * slot_rows).reshape(slot_count + 4, slot_rows, channels)
    mixed_rows = temporal_mix(padded, clip_mask, kernel_full, slot_count).reshape(tokens, channels)
    features = (stem_out + jax.nn.silu(mixed_rows)).astype(jnp.bfloat16)
    upstream_wide = cotangent[0].astype(jnp.float32)
    gate_value = jax.nn.sigmoid(mixed_rows)
    slope_low = (upstream_wide * gate_value * (1.0 + mixed_rows * (1.0 - gate_value))).astype(
        jnp.bfloat16
    )
    slope_padded = rim_rows(slope_low, 2 * slot_rows).reshape(slot_count + 4, slot_rows, channels)
    d_normed = temporal_back(slope_padded, mask_padded, kernel_full, slot_count).reshape(
        tokens, channels
    )
    gated = d_normed * gain_wide
    d_stem = upstream_wide + inv_rms * (
        gated - unit_rows * jnp.mean(gated * unit_rows, axis=1, keepdims=True)
    )
    d_stem_low = d_stem.astype(jnp.bfloat16)
    grad_rows = jnp.dot(d_stem_low, weight_full, preferred_element_type=jnp.float32).astype(
        jnp.bfloat16
    )
    gain_part = jnp.sum(d_normed * unit_rows, axis=0)
    slope_blocks = slope_padded[2 : 2 + slot_count]
    kernel_part = kernel_sums(slope_blocks, padded, clip_mask, slot_count)
    chan_terms = jnp.concatenate([gain_part[None, :], kernel_part], axis=0).T
    weight_block = lax.dot_general(
        d_stem_low, packed, (((0,), (0,)), ((), ())), preferred_element_type=jnp.float32
    )
    grad_shard = lax.psum_scatter(
        jnp.concatenate([weight_block, chan_terms], axis=1), "fsdp", scatter_dimension=0, tiled=True
    )
    summed = lax.psum(grad_shard, "seq")
    grad_scale = 1.0 / math.sqrt(tokens * seq_size * fsdp_size)
    grad_weight = (summed[:, :pixel_width] * grad_scale).astype(jnp.bfloat16)
    grad_channels = (summed[:, pixel_width:] * grad_scale).T
    return (features[None], grad_rows[None], grad_weight, grad_channels)


def solution(mesh):
    in_specs = (
        P("fsdp", "seq", None),
        P("fsdp", "seq"),
        P("fsdp", None),
        P("fsdp", None),
        P("fsdp"),
        P(None, "fsdp"),
        P("fsdp", "seq", None),
    )
    out_specs = (P("fsdp", "seq", None), P("fsdp", "seq", None), P("fsdp", None), P(None, "fsdp"))
    return jax.shard_map(shards, mesh=mesh, in_specs=in_specs, out_specs=out_specs, check_vma=False)
```

profile of v0, /device:TPU:32, one launch (start us, length us, event | category | flops | bytes accessed | tf_op | source)
XLA Modules:
  0.0 471.1 jit_solution(15271871692152045158)
XLA Ops:
  9.3 0.9 convert_reduce_fusion
  12.2 7.0 %all-to-all-start = ((bf16[16,2,1]{1,2,0:T(2,128)(2,1)}), bf16[16,2,1]{1,2,0:T(2,128)(2,1)S(1)}, u32[]{:S(2)}, u32[]{:S(2)}) async-start(bf16[16,2,1]{1,2,0:T(2,128)(2,1)} %all_to_all.12), calls=%async_computation | async-start | bytes 16384 | tf_op jit(solution)/shard_map/all_to_all | solution.py:113
  19.3 0.7 gather_fusion.5
  20.0 0.7 gather_fusion.6
  20.8 0.7 gather_fusion.8
  21.5 0.7 gather_fusion.7
  23.0 18.3 %all-gather = bf16[16,224,5]{1,2,0:T(8,128)(2,1)S(1)} all-gather(bf16[1,224,5]{1,2,0:T(8,128)(2,1)} %bitcast.126), channel_id=1, replica_groups=mesh['seq'=16,'fsdp'=16] {'fsdp'}, dimensions={0}, use_global_device_ids=true | all-gather | bytes 38080 | tf_op jit(solution)/shard_map/all_gather | solution.py:126
  45.6 0.8 broadcast_multiply_fusion
  46.4 0.9 broadcast_multiply_fusion.1
  47.4 1.8 broadcast_in_dim.19
  49.2 5.8 %scatter_fusion = bf16[32,32,1176]{2,1,0:T(8,128)(2,1)} fusion(bf16[32,32,1176]{2,1,0:T(8,128)(2,1)} %broadcast_in_dim.19, s32[17]{0:T(128)S(1)} %fusion.26, bf16[17,32,1176]{2,1,0:T(8,128)(2,1)S(1)} %bitcast.120), kind=kCustom, calls=%fused_computation.11 | custom fusion | bytes 3838532 | tf_op jit(solution)/shard_map/scatter | solution.py:103
  55.0 7.3 %all-to-all-start.1 = ((bf16[32,32,1176]{2,1,0:T(8,128)(2,1)}), bf16[32,32,1176]{2,1,0:T(8,128)(2,1)}, u32[]{:S(2)}, u32[]{:S(2)}) async-start(bf16[32,32,1176]{2,1,0:T(8,128)(2,1)} %scatter_fusion), calls=%async_computation.1 | async-start | bytes 5242880 | tf_op jit(solution)/shard_map/all_to_all | solution.py:112
  63.9 24.1 %all-reduce = bf16[3584]{0:T(1024)(128)(2,1)S(1)} all-reduce(bf16[3584]{0:T(1024)(128)(2,1)S(1)} %dynamic-update-slice), channel_id=1, replica_groups=mesh['seq'=16,'fsdp'=16] {'fsdp'}, use_global_device_ids=true, to_apply=%add | all-reduce | flops 3584 | bytes 14336
  88.1 1.0 broadcast_multiply_fusion.2
  89.0 1.0 broadcast_multiply_fusion.3
  90.1 8.8 %all-to-all-done.1 = bf16[32,32,1176]{2,1,0:T(8,128)(2,1)} async-done(((bf16[32,32,1176]{2,1,0:T(8,128)(2,1)}), bf16[32,32,1176]{2,1,0:T(8,128)(2,1)}, u32[]{:S(2)}, u32[]{:S(2)}) %all-to-all-start.1) | async-done | bytes 2408480 | tf_op jit(solution)/shard_map/all_to_all | solution.py:112
  99.1 4.2 scatter_fusion.1
  103.4 8.0 %multiply_reduce_fusion.2 = (f32[544]{0:T(1024)S(1)}, f32[544,3584]{1,0:T(8,128)S(1)}) fusion(bf16[544,1176]{1,0:T(8,128)(2,1)S(1)} %bitcast.121, bf16[3584,1176]{1,0:T(8,128)(2,1)} %all-gather.3.cloned.1.call-done), kind=kOutput, calls=%fused_computation.47 | convolution fusion | flops 4589583872 | bytes 17510016 | tf_op jit(solution)/shard_map/dot_general | solution.py:130
  111.5 1.3 multiply_convert_fusion
  112.9 1.6 collective-permute-start.1
  114.5 4.8 %collective-permute-start = (bf16[64,3584]{1,0:T(8,128)(2,1)S(1)}, bf16[64,3584]{1,0:T(8,128)(2,1)S(1)}, u32[]{:S(2)}, u32[]{:S(2)}) collective-permute-start(bf16[64,3584]{1,0:T(8,128)(2,1)S(1)} %get-tuple-element.46), channel_id=1, source_target_pairs={{0,16},{16,32},{32,48},{48,64},{64,80},{80,96},{96,112},{112,128},... | collective-permute-start | bytes 1376264 | tf_op jit(solution)/shard_map/ppermute | solution.py:18
  119.3 0.9 broadcast_multiply_fusion.4
  120.2 5.8 %collective-permute-done.1 = bf16[64,3584]{1,0:T(8,128)(2,1)S(1)} collective-permute-done((bf16[64,3584]{1,0:T(8,128)(2,1)S(1)}, bf16[64,3584]{1,0:T(8,128)(2,1)S(1)}, u32[]{:S(2)}, u32[]{:S(2)}) %collective-permute-start.1) | collective-permute-done | bytes 458784 | tf_op jit(solution)/shard_map/ppermute | solution.py:20
  126.0 1.3 collective-permute-done
  127.4 8.3 %convert_multiply_fusion = (f32[544,3584]{1,0:T(8,128)}, bf16[544,3584]{1,0:T(8,128)(2,1)S(1)}, f32[544,3584]{1,0:T(8,128)}) fusion(bf16[64,3584]{1,0:T(8,128)(2,1)S(1)} %collective-permute-done.1, bf16[544,3584]{1,0:T(8,128)(2,1)S(1)} %multiply_convert_fusion, bf16[1,544,3584]{2,1,0:T(8,128)(2,1)S(1)} %copy-done.5, f32[17,3584]{1,0:T(8,128)S(1)} %copy-done.7, ...), kind=kLoop, calls=%fused_computation.13 | loop fusion | flops 74088448 | bytes 29431808 | tf_op jit(solution)/shard_map/mul | solution.py:72
  135.7 1.9 copy-done.3
  137.6 0.8 fusion.45
  138.4 5.5 %collective-permute-start.3 = (bf16[64,3584]{1,0:T(8,128)(2,1)}, bf16[64,3584]{1,0:T(8,128)(2,1)}, u32[]{:S(2)}, u32[]{:S(2)}) collective-permute-start(bf16[64,3584]{1,0:T(8,128)(2,1)} %get-tuple-element.45), channel_id=1, source_target_pairs={{0,16},{16,32},{32,48},{48,64},{64,80},{80,96},{96,112},{112,128},... | collective-permute-start | bytes 1376264 | tf_op jit(solution)/shard_map/ppermute | solution.py:18
  143.9 1.5 collective-permute-start.2
  145.4 15.1 %convert_multiply_fusion.1 = (f32[544,3584]{1,0:T(8,128)}, f32[544,3584]{1,0:T(8,128)}, f32[544,3584]{1,0:T(8,128)}, f32[544,3584]{1,0:T(8,128)}) fusion(bf16[544,3584]{1,0:T(8,128)(2,1)} %copy-done.3, bf16[64,3584]{1,0:T(8,128)(2,1)S(1)} %collective-permute-done.1, bf16[544,3584]{1,0:T(8,128)(2,1)} %copy-done.4, bf16[64,3584]{1,0:T(8,128)(2,1)S(1)} %collective-permute-done), kind=kLoop, calls=%fused_computation.14 | loop fusion | flops 35094528 | bytes 39911424 | tf_op jit(solution)/shard_map/mul | solution.py:72
  160.5 4.3 reduce_sum.133
  165.0 4.4 reduce_sum.135
  169.5 4.4 reduce_sum.137
  174.0 4.4 reduce_sum.139
  178.5 4.4 reduce_sum.141
  183.0 10.2 %fusion.9 = f32[544,3584]{1,0:T(8,128)S(1)} fusion(bf16[544,3584]{1,0:T(8,128)(2,1)} %copy-done.3, bf16[64,3584]{1,0:T(8,128)(2,1)} %collective-permute-done.3, bf16[64,3584]{1,0:T(8,128)(2,1)} %collective-permute-done.2, f32[17,3584]{1,0:T(8,128)S(1)} %get-tuple-element.56, f32[17,3584]{1,0:T(8,128)} %get-tuple-element.54, ...), kind=kLoop, calls=%fused_computation.36 | loop fusion | flops 50692096 | bytes 13834240 | tf_op jit(solution)/shard_map/add | solution.py:62
  193.3 2.1 multiply_reduce_fusion
  195.4 9.9 %fusion.6 = (bf16[544,3584]{1,0:T(8,128)(2,1)}, bf16[1,544,3584]{2,1,0:T(8,128)(2,1)}) fusion(f32[544,3584]{1,0:T(8,128)S(1)} %fusion.9, f32[544,3584]{1,0:T(8,128)S(1)} %bitcast.114, bf16[1,544,3584]{2,1,0:T(8,128)(2,1)} %param.13, f32[544]{0:T(1024)S(1)} %broadcast_multiply_fusion.10, f32[3584]{0:T(1024)S(1)} %convert_element_type.185, ...), kind=kLoop, calls=%fused_computation.33 | loop fusion | flops 27295744 | bytes 35113216 | tf_op jit(solution)/shard_map/convert_element_type | solution.py:157
  205.3 12.7 %fusion.47 = f32[3584,1176]{0,1:T(8,128)} fusion(bf16[544,3584]{1,0:T(8,128)(2,1)} %get-tuple-element.42, bf16[544,1176]{1,0:T(8,128)(2,1)S(1)} %bitcast.122), kind=kOutput, calls=%fused_computation.172 | convolution fusion | flops 4585684992 | bytes 22038016 | tf_op jit(solution)/shard_map/dot_general | solution.py:165
  218.1 11.5 %pad_maximum_fusion = f32[3584,1182]{0,1:T(8,128)} fusion(f32[3584,6]{0,1:T(8,128)S(1)} %bitcast.123, f32[3584,1176]{0,1:T(8,128)} %fusion.47), kind=kLoop, calls=%fused_computation.19 | loop fusion | flops 4236288 | bytes 33890304 | tf_op jit(solution)/shard_map/concatenate | solution.py:169
  229.6 18.8 %copy.23 = f32[3584,1182]{1,0:T(8,128)} copy(f32[3584,1182]{0,1:T(8,128)} %pad_maximum_fusion) | data formatting | bytes 33890304
  248.5 109.9 %reduce-scatter.4.cloned.1.call-done = f32[224,1182]{1,0:T(8,128)} async-done(((f32[3584,1182]{1,0:T(8,128)}), f32[224,1182]{1,0:T(8,128)}) %reduce-scatter.4.cloned.1.call-update) | async-done | bytes 1059088
  358.4 2.7 copy.24
  361.1 10.4 %fusion.16 = bf16[1,544,1176]{2,1,0:T(8,128)(2,1)} fusion(bf16[544,3584]{1,0:T(8,128)(2,1)} %get-tuple-element.42, bf16[3584,1176]{1,0:T(8,128)(2,1)} %all-gather.3.cloned.1.call-done), kind=kOutput, calls=%fused_computation.66 | convolution fusion | flops 4586324992 | bytes 13608448 | tf_op jit(solution)/shard_map/dot_general | solution.py:158
  371.5 89.3 %all-reduce.3.cloned.1.call-done = f32[224,1182]{0,1:T(8,128)} async-done(((f32[224,1182]{0,1:T(8,128)}), f32[224,1182]{0,1:T(8,128)}) %all-reduce.3.cloned.1.call-update) | async-done | bytes 1059088 | tf_op jit(solution)/shard_map/psum | solution.py:171
  460.8 1.4 fusion.17
  462.2 1.0 copy.22
  463.3 1.3 fusion.18
  (107 shorter events, 11.4 us)
Async XLA Ops:
  7.2 12.1 %copy-start = (s32[1,272]{1,0:T(1,128)S(1)}, s32[1,272]{1,0:T(1,128)}, u32[]{:S(2)}) copy-start(s32[1,272]{1,0:T(1,128)} %param.9) | copy-start | bytes 3268
  7.2 42.0 %copy-start.6 = (bf16[1,544,1176]{2,1,0:T(8,128)(2,1)S(1)}, bf16[1,544,1176]{2,1,0:T(8,128)(2,1)}, u32[]{:S(2)}) copy-start(bf16[1,544,1176]{2,1,0:T(8,128)(2,1)} %param.7) | copy-start | bytes 3838468
  7.2 96.2 %all-gather.3.cloned.1.call-start = ((), (), s32[]{:S(2)}) async-start(), calls=%async_computation.3 | async-start | bytes 9748480 | tf_op jit(solution)/shard_map/all_gather | solution.py:124
  12.2 42.8 %all-to-all-start = ((bf16[16,2,1]{1,2,0:T(2,128)(2,1)}), bf16[16,2,1]{1,2,0:T(2,128)(2,1)S(1)}, u32[]{:S(2)}, u32[]{:S(2)}) async-start(bf16[16,2,1]{1,2,0:T(2,128)(2,1)} %all_to_all.12), calls=%async_computation | async-start | bytes 16384 | tf_op jit(solution)/shard_map/all_to_all | solution.py:113
  42.2 20.2 %copy-start.12 = (u32[256]{0:T(256)S(1)}, u32[256]{0:T(256)}, u32[]{:S(2)}) copy-start(u32[256]{0:T(256)} %constant.79) | copy-start | bytes 3076
  42.2 21.5 %copy-start.11 = (bf16[224]{0:T(256)(128)(2,1)S(1)}, bf16[224]{0:T(256)(128)(2,1)}, u32[]{:S(2)}) copy-start(bf16[224]{0:T(256)(128)(2,1)} %param.11) | copy-start | bytes 1348
  55.0 43.9 %all-to-all-start.1 = ((bf16[32,32,1176]{2,1,0:T(8,128)(2,1)}), bf16[32,32,1176]{2,1,0:T(8,128)(2,1)}, u32[]{:S(2)}, u32[]{:S(2)}) async-start(bf16[32,32,1176]{2,1,0:T(8,128)(2,1)} %scatter_fusion), calls=%async_computation.1 | async-start | bytes 5242880 | tf_op jit(solution)/shard_map/all_to_all | solution.py:112
  62.3 296.1 %reduce-scatter.4.cloned.1.call-start = ((), (), s32[]{:S(2)}) async-start(), calls=%async_computation.5 | async-start | bytes 19496960
  111.4 24.2 %copy-start.2 = (f32[544,3584]{1,0:T(8,128)}, f32[544,3584]{1,0:T(8,128)S(1)}, u32[]{:S(2)}) copy-start(f32[544,3584]{1,0:T(8,128)S(1)} %get-tuple-element.69) | copy-start | bytes 23396356
  111.4 15.9 %copy-start.5 = (bf16[1,544,3584]{2,1,0:T(8,128)(2,1)S(1)}, bf16[1,544,3584]{2,1,0:T(8,128)(2,1)}, u32[]{:S(2)}) copy-start(bf16[1,544,3584]{2,1,0:T(8,128)(2,1)} %param.13) | copy-start | bytes 11698180
  111.5 15.9 %copy-start.7 = (f32[17,3584]{1,0:T(8,128)S(1)}, f32[17,3584]{1,0:T(8,128)}, u32[]{:S(2)}) copy-start(f32[17,3584]{1,0:T(8,128)} %get-tuple-element.57) | copy-start | bytes 731140
  111.5 15.9 %copy-start.8 = (f32[17,3584]{1,0:T(8,128)S(1)}, f32[17,3584]{1,0:T(8,128)}, u32[]{:S(2)}) copy-start(f32[17,3584]{1,0:T(8,128)} %get-tuple-element.55) | copy-start | bytes 731140
  111.5 15.9 %copy-start.9 = (f32[17,3584]{1,0:T(8,128)S(1)}, f32[17,3584]{1,0:T(8,128)}, u32[]{:S(2)}) copy-start(f32[17,3584]{1,0:T(8,128)} %get-tuple-element.53) | copy-start | bytes 731140
  111.5 15.9 %copy-start.10 = (f32[17,3584]{1,0:T(8,128)S(1)}, f32[17,3584]{1,0:T(8,128)}, u32[]{:S(2)}) copy-start(f32[17,3584]{1,0:T(8,128)} %get-tuple-element.51) | copy-start | bytes 731140
  112.8 22.9 %copy-start.4 = (bf16[544,3584]{1,0:T(8,128)(2,1)}, bf16[544,3584]{1,0:T(8,128)(2,1)S(1)}, u32[]{:S(2)}) copy-start(bf16[544,3584]{1,0:T(8,128)(2,1)S(1)} %multiply_convert_fusion) | copy-start | bytes 11698180
  112.9 13.1 %collective-permute-start.1 = (bf16[64,3584]{1,0:T(8,128)(2,1)S(1)}, bf16[64,3584]{1,0:T(8,128)(2,1)S(1)}, u32[]{:S(2)}, u32[]{:S(2)}) collective-permute-start(bf16[64,3584]{1,0:T(8,128)(2,1)S(1)} %get-tuple-element.47), channel_id=1, source_target_pairs={{16,0},{32,16},{48,32},{64,48},{80,64},{96,80},{112,96},{128,112},... | collective-permute-start | bytes 1376264 | tf_op jit(solution)/shard_map/ppermute | solution.py:20
  114.5 12.9 %collective-permute-start = (bf16[64,3584]{1,0:T(8,128)(2,1)S(1)}, bf16[64,3584]{1,0:T(8,128)(2,1)S(1)}, u32[]{:S(2)}, u32[]{:S(2)}) collective-permute-start(bf16[64,3584]{1,0:T(8,128)(2,1)S(1)} %get-tuple-element.46), channel_id=1, source_target_pairs={{0,16},{16,32},{32,48},{48,64},{64,80},{80,96},{96,112},{112,128},... | collective-permute-start | bytes 1376264 | tf_op jit(solution)/shard_map/ppermute | solution.py:18
  135.7 1.9 copy-start.3
  138.4 44.6 %collective-permute-start.3 = (bf16[64,3584]{1,0:T(8,128)(2,1)}, bf16[64,3584]{1,0:T(8,128)(2,1)}, u32[]{:S(2)}, u32[]{:S(2)}) collective-permute-start(bf16[64,3584]{1,0:T(8,128)(2,1)} %get-tuple-element.45), channel_id=1, source_target_pairs={{0,16},{16,32},{32,48},{48,64},{64,80},{80,96},{96,112},{112,128},... | collective-permute-start | bytes 1376264 | tf_op jit(solution)/shard_map/ppermute | solution.py:18
  143.9 39.1 %collective-permute-start.2 = (bf16[64,3584]{1,0:T(8,128)(2,1)S(1)}, bf16[64,3584]{1,0:T(8,128)(2,1)}, u32[]{:S(2)}, u32[]{:S(2)}) collective-permute-start(bf16[64,3584]{1,0:T(8,128)(2,1)S(1)} %get-tuple-element.44), channel_id=1, source_target_pairs={{16,0},{32,16},{48,32},{64,48},{80,64},{96,80},{112,96},{128,112},... | collective-permute-start | bytes 1376264 | tf_op jit(solution)/shard_map/ppermute | solution.py:20
  182.8 10.4 %slice-start = ((s8[7798784]{0:T(1024)(128)(4,1)}), s8[4194304]{0:T(1024)(128)(4,1)S(1)}, s32[]{:S(2)}) async-start(s8[7798784]{0:T(1024)(128)(4,1)} %bitcast.113), calls=%async_computation.6 | async-start | bytes 8388608
  183.0 10.3 %slice-start.1 = ((s8[7798784]{0:T(1024)(128)(4,1)}), s8[3604480]{0:T(1024)(128)(4,1)S(1)}, s32[]{:S(2)}) async-start(s8[7798784]{0:T(1024)(128)(4,1)} %bitcast.113), calls=%async_computation.7 | async-start | bytes 7208960
  248.5 212.3 %all-reduce.3.cloned.1.call-start = ((), (), s32[]{:S(2)}) async-start(), calls=%async_computation.4 | async-start | bytes 2424832 | tf_op jit(solution)/shard_map/psum | solution.py:171
  361.1 103.5 %copy-start.1 = (s32[1,272]{1,0:T(1,128)S(1)}, s32[1,272]{1,0:T(1,128)}, u32[]{:S(2)}) copy-start(s32[1,272]{1,0:T(1,128)} %param.9) | copy-start | bytes 3268
Sparse Core Ops, SparseCore 0:
  9.9 60.7 all-gather.2
  248.6 109.7 reduce-scatter.3
  361.7 99.0 all-reduce.2
where the time goes:
time: 472 us; the launch traced here: 471 us
  waiting for transfers between devices  216 us (46%)
  other arithmetic  91.6 us (19%)
  local copies, waits for them, and re-layouts  47.3 us (10%)
  blocking collectives  42.4 us (9%)
  matrix products  31.1 us (7%)
  starting transfers between devices  27.8 us (6%)
  between operations  15 us (3%)
    unnamed x4, waiting for transfers between devices  111 us
    psum x1, waiting for transfers between devices, shards(): summed = lax.psum(grad_shard, 'seq')  89.3 us
    unnamed x36, local copies, waits for them, and re-layouts  25.4 us
    unnamed x1, blocking collectives  24.1 us
    mul x2, other arithmetic, kernel_sums(): slope_blocks.astype(jnp.float32)  23.4 us
    reduce_sum x5, other arithmetic, kernel_sums(): jnp.sum(slope_blocks.astype(jnp.float32) * padded[offset:offset + slot_to...  21.8 us
    all_gather x1, blocking collectives, shards(): lax.all_gather(conv_kernel, 'fsdp', axis=1, tiled=True)  18.3 us
    dot_general x1, matrix products, shards(): lax.dot_general(d_stem_low, packed, (((0,), (0,)), ((), ())), preferred_e...  12.7 us
  transfers between devices with their start and end apart: 9, of which 5 were waited for; matrix products, arithmetic and copies ran while one was open for 16% of the time, Pallas kernels for 0%

commit v1 on v0

--- a/solution.py
+++ b/solution.py
@@ -120,10 +120,19 @@
         .set(incoming)[:slot_count]
         .reshape(tokens, pixel_width)
     )
+    _pass_lines = lambda inp, device_axis: jnp.concatenate(
+        jax.lax.all_to_all(
+            jnp.stack([inp for _ in range(jax.lax.psum(1, axis_name=device_axis))]),
+            axis_name=device_axis,
+            split_axis=0,
+            concat_axis=0,
+        ),
+        axis=1,
+    )
     weight_full, gain_low, kernel_full = (
         lax.all_gather(stem_weight, "fsdp", axis=0, tiled=True),
         lax.all_gather(norm_gain, "fsdp", axis=0, tiled=True),
-        lax.all_gather(conv_kernel, "fsdp", axis=1, tiled=True),
+        _pass_lines(conv_kernel, "fsdp"),
     )
     gain_wide = gain_low.astype(jnp.float32)
     channels = weight_full.shape[0]

time: 472 us -> 495 us (1.049)
  waiting for transfers between devices: 216 us -> 243 us
  blocking collectives: 42.4 us -> 27.5 us
  starting transfers between devices: 27.8 us -> 35.3 us
    all_to_all x1, waiting for transfers between devices: 8.8 us -> 32.1 us  [shards(): lax.all_to_all(outbox, 'seq', split_axis=0, concat_axis=0, tiled=True)]
    all_gather x1 -> x0, blocking collectives: 18.3 us -> none  [shards(): lax.all_gather(conv_kernel, 'fsdp', axis=1, tiled=True)]
    all_to_all x0 -> x1, starting transfers between devices: none -> 7.84 us  [shards(): jax.lax.all_to_all(jnp.stack([inp for _ in range(jax.lax.psum(1, axis_nam...]
    all_to_all x0 -> x1, waiting for transfers between devices: none -> 6.39 us  [shards(): jax.lax.all_to_all(jnp.stack([inp for _ in range(jax.lax.psum(1, axis_nam...]
    unnamed x36 -> x34, local copies, waits for them, and re-layouts: 25.4 us -> 26.7 us
  transfers between devices with their start and end apart: 9 -> 10, of which waited for: 5 -> 6; matrix products, arithmetic and copies ran while one was open for 16% -> 16% of each run, Pallas kernels for 0% -> 0%
where the time goes in v1:
time: 495 us; the launch traced here: 493 us
  waiting for transfers between devices  243 us (49%)
  other arithmetic  91.6 us (19%)
  local copies, waits for them, and re-layouts  49.6 us (10%)
  starting transfers between devices  35.3 us (7%)
  matrix products  31.2 us (6%)
  blocking collectives  27.5 us (6%)
  between operations  15 us (3%)
    unnamed x4, waiting for transfers between devices  109 us
    psum x1, waiting for transfers between devices, shards(): summed = lax.psum(grad_shard, 'seq')  89.2 us
    all_to_all x1, waiting for transfers between devices, shards(): lax.all_to_all(outbox, 'seq', split_axis=0, concat_axis=0, tiled=True)  32.1 us
    unnamed x1, blocking collectives  27.5 us
    unnamed x34, local copies, waits for them, and re-layouts  26.7 us
    mul x2, other arithmetic, kernel_sums(): slope_blocks.astype(jnp.float32)  23.4 us
    reduce_sum x5, other arithmetic, kernel_sums(): jnp.sum(slope_blocks.astype(jnp.float32) * padded[offset:offset + slot_to...  21.8 us
    dot_general x1, matrix products, shards(): lax.dot_general(d_stem_low, packed, (((0,), (0,)), ((), ())), preferred_e...  12.7 us
  transfers between devices with their start and end apart: 10, of which 6 were waited for; matrix products, arithmetic and copies ran while one was open for 16% of the time, Pallas kernels for 0%

profile of v1, /device:TPU:32, one launch (start us, length us, event | category | flops | bytes accessed | tf_op | source)
XLA Modules:
  0.0 493.5 jit_solution(14948342749397299157)
XLA Ops:
  9.3 0.9 convert_reduce_fusion
  12.2 7.0 %all-to-all-start = ((bf16[16,2,1]{1,2,0:T(2,128)(2,1)}), bf16[16,2,1]{1,2,0:T(2,128)(2,1)S(1)}, u32[]{:S(2)}, u32[]{:S(2)}) async-start(bf16[16,2,1]{1,2,0:T(2,128)(2,1)} %all_to_all.16), calls=%async_computation | async-start | bytes 16384 | tf_op jit(solution)/shard_map/all_to_all | solution.py:113
  19.3 1.3 dynamic-slice
  21.2 0.9 dynamic-update-slice
  22.0 27.5 %all-reduce = bf16[3584]{0:T(1024)(128)(2,1)S(1)} all-reduce(bf16[3584]{0:T(1024)(128)(2,1)S(1)} %dynamic-update-slice), channel_id=1, replica_groups=mesh['seq'=16,'fsdp'=16] {'fsdp'}, use_global_device_ids=true, to_apply=%add | all-reduce | flops 3584 | bytes 14336
  49.7 0.7 gather_fusion.5
  57.3 1.8 broadcast_in_dim.19
  59.1 5.9 %scatter_fusion = bf16[32,32,1176]{2,1,0:T(8,128)(2,1)} fusion(bf16[32,32,1176]{2,1,0:T(8,128)(2,1)} %broadcast_in_dim.19, s32[17]{0:T(128)S(1)} %fusion.26, bf16[17,32,1176]{2,1,0:T(8,128)(2,1)S(1)} %bitcast.116), kind=kCustom, calls=%fused_computation.11 | custom fusion | bytes 3838532 | tf_op jit(solution)/shard_map/scatter | solution.py:103
  65.6 7.8 %all-to-all-start.2 = ((bf16[16,5,224]{2,1,0:T(8,128)(2,1)}), bf16[16,5,224]{2,1,0:T(8,128)(2,1)S(1)}, u32[]{:S(2)}, u32[]{:S(2)}) async-start(bf16[16,5,224]{2,1,0:T(8,128)(2,1)} %stack.12), calls=%async_computation.2 | async-start | bytes 131072 | tf_op jit(solution)/shard_map/all_to_all | solution.py:124
  73.6 6.4 %all-to-all-done.2 = bf16[16,5,224]{2,1,0:T(8,128)(2,1)S(1)} async-done(((bf16[16,5,224]{2,1,0:T(8,128)(2,1)}), bf16[16,5,224]{2,1,0:T(8,128)(2,1)S(1)}, u32[]{:S(2)}, u32[]{:S(2)}) %all-to-all-start.2) | async-done | bytes 35872 | tf_op jit(solution)/shard_map/all_to_all | solution.py:124
  80.0 7.3 %all-to-all-start.1 = ((bf16[32,32,1176]{2,1,0:T(8,128)(2,1)}), bf16[32,32,1176]{2,1,0:T(8,128)(2,1)}, u32[]{:S(2)}, u32[]{:S(2)}) async-start(bf16[32,32,1176]{2,1,0:T(8,128)(2,1)} %scatter_fusion), calls=%async_computation.1 | async-start | bytes 5242880 | tf_op jit(solution)/shard_map/all_to_all | solution.py:112
  87.7 0.8 broadcast_multiply_fusion
  88.5 0.9 broadcast_multiply_fusion.1
  89.7 1.0 broadcast_multiply_fusion.2
  90.7 1.0 broadcast_multiply_fusion.3
  91.7 32.1 %all-to-all-done.1 = bf16[32,32,1176]{2,1,0:T(8,128)(2,1)} async-done(((bf16[32,32,1176]{2,1,0:T(8,128)(2,1)}), bf16[32,32,1176]{2,1,0:T(8,128)(2,1)}, u32[]{:S(2)}, u32[]{:S(2)}) %all-to-all-start.1) | async-done | bytes 2408480 | tf_op jit(solution)/shard_map/all_to_all | solution.py:112
  124.0 4.2 scatter_fusion.1
  128.3 8.0 %multiply_reduce_fusion.2 = (f32[544]{0:T(1024)S(1)}, f32[544,3584]{1,0:T(8,128)S(1)}) fusion(bf16[544,1176]{1,0:T(8,128)(2,1)S(1)} %bitcast.117, bf16[3584,1176]{1,0:T(8,128)(2,1)} %all-gather.2.cloned.1.call-done), kind=kOutput, calls=%fused_computation.47 | convolution fusion | flops 4589583872 | bytes 17510016 | tf_op jit(solution)/shard_map/dot_general | solution.py:139
  136.4 1.3 multiply_convert_fusion
  137.8 1.6 collective-permute-start.1
  139.3 4.8 collective-permute-start
  144.2 0.9 broadcast_multiply_fusion.4
  145.1 5.7 %collective-permute-done.1 = bf16[64,3584]{1,0:T(8,128)(2,1)S(1)} collective-permute-done((bf16[64,3584]{1,0:T(8,128)(2,1)S(1)}, bf16[64,3584]{1,0:T(8,128)(2,1)S(1)}, u32[]{:S(2)}, u32[]{:S(2)}) %collective-permute-start.1) | collective-permute-done | bytes 458784 | tf_op jit(solution)/shard_map/ppermute | solution.py:20
  150.7 1.3 collective-permute-done
  152.1 8.3 %convert_multiply_fusion = (f32[544,3584]{1,0:T(8,128)}, bf16[544,3584]{1,0:T(8,128)(2,1)S(1)}, f32[544,3584]{1,0:T(8,128)}) fusion(bf16[64,3584]{1,0:T(8,128)(2,1)S(1)} %collective-permute-done.1, bf16[544,3584]{1,0:T(8,128)(2,1)S(1)} %multiply_convert_fusion, bf16[1,544,3584]{2,1,0:T(8,128)(2,1)S(1)} %copy-done.5, f32[17,3584]{1,0:T(8,128)S(1)} %copy-done.7, ...), kind=kLoop, calls=%fused_computation.13 | loop fusion | flops 74088448 | bytes 29431808 | tf_op jit(solution)/shard_map/mul | solution.py:72
  160.4 1.9 copy-done.3
  162.3 0.8 fusion.45
  163.1 5.2 %collective-permute-start.3 = (bf16[64,3584]{1,0:T(8,128)(2,1)}, bf16[64,3584]{1,0:T(8,128)(2,1)}, u32[]{:S(2)}, u32[]{:S(2)}) collective-permute-start(bf16[64,3584]{1,0:T(8,128)(2,1)} %get-tuple-element.41), channel_id=1, source_target_pairs={{0,16},{16,32},{32,48},{48,64},{64,80},{80,96},{96,112},{112,128},... | collective-permute-start | bytes 1376264 | tf_op jit(solution)/shard_map/ppermute | solution.py:18
  168.4 1.5 collective-permute-start.2
  169.8 15.1 %convert_multiply_fusion.1 = (f32[544,3584]{1,0:T(8,128)}, f32[544,3584]{1,0:T(8,128)}, f32[544,3584]{1,0:T(8,128)}, f32[544,3584]{1,0:T(8,128)}) fusion(bf16[544,3584]{1,0:T(8,128)(2,1)} %copy-done.3, bf16[64,3584]{1,0:T(8,128)(2,1)S(1)} %collective-permute-done.1, bf16[544,3584]{1,0:T(8,128)(2,1)} %copy-done.4, bf16[64,3584]{1,0:T(8,128)(2,1)S(1)} %collective-permute-done), kind=kLoop, calls=%fused_computation.14 | loop fusion | flops 35094528 | bytes 39911424 | tf_op jit(solution)/shard_map/mul | solution.py:72
  184.9 4.3 reduce_sum.133
  189.4 4.4 reduce_sum.135
  193.9 4.4 reduce_sum.137
  198.4 4.4 reduce_sum.139
  202.9 4.4 reduce_sum.141
  207.5 10.2 %fusion.9 = f32[544,3584]{1,0:T(8,128)S(1)} fusion(bf16[544,3584]{1,0:T(8,128)(2,1)} %copy-done.3, bf16[64,3584]{1,0:T(8,128)(2,1)} %collective-permute-done.3, bf16[64,3584]{1,0:T(8,128)(2,1)} %collective-permute-done.2, f32[17,3584]{1,0:T(8,128)S(1)} %get-tuple-element.52, f32[17,3584]{1,0:T(8,128)} %get-tuple-element.50, ...), kind=kLoop, calls=%fused_computation.36 | loop fusion | flops 50692096 | bytes 13834240 | tf_op jit(solution)/shard_map/add | solution.py:62
  217.7 2.1 multiply_reduce_fusion
  219.8 9.9 %fusion.6 = (bf16[544,3584]{1,0:T(8,128)(2,1)}, bf16[1,544,3584]{2,1,0:T(8,128)(2,1)}) fusion(f32[544,3584]{1,0:T(8,128)S(1)} %fusion.9, f32[544,3584]{1,0:T(8,128)S(1)} %bitcast.110, bf16[1,544,3584]{2,1,0:T(8,128)(2,1)} %param.13, f32[544]{0:T(1024)S(1)} %broadcast_multiply_fusion.10, f32[3584]{0:T(1024)S(1)} %convert_element_type.189, ...), kind=kLoop, calls=%fused_computation.33 | loop fusion | flops 27295744 | bytes 35113216 | tf_op jit(solution)/shard_map/convert_element_type | solution.py:166
  229.7 12.7 %fusion.47 = f32[3584,1176]{0,1:T(8,128)} fusion(bf16[544,3584]{1,0:T(8,128)(2,1)} %get-tuple-element.38, bf16[544,1176]{1,0:T(8,128)(2,1)S(1)} %bitcast.118), kind=kOutput, calls=%fused_computation.172 | convolution fusion | flops 4585684992 | bytes 22038016 | tf_op jit(solution)/shard_map/dot_general | solution.py:174
  242.6 11.5 %pad_maximum_fusion = f32[3584,1182]{0,1:T(8,128)} fusion(f32[3584,6]{0,1:T(8,128)S(1)} %bitcast.119, f32[3584,1176]{0,1:T(8,128)} %fusion.47), kind=kLoop, calls=%fused_computation.19 | loop fusion | flops 4236288 | bytes 33890304 | tf_op jit(solution)/shard_map/concatenate | solution.py:178
  254.1 18.8 %copy.17 = f32[3584,1182]{1,0:T(8,128)} copy(f32[3584,1182]{0,1:T(8,128)} %pad_maximum_fusion) | data formatting | bytes 33890304
  273.0 107.9 %reduce-scatter.4.cloned.1.call-done = f32[224,1182]{1,0:T(8,128)} async-done(((f32[3584,1182]{1,0:T(8,128)}), f32[224,1182]{1,0:T(8,128)}) %reduce-scatter.4.cloned.1.call-update) | async-done | bytes 1059088
  380.8 2.7 copy.18
  383.6 10.4 %fusion.16 = bf16[1,544,1176]{2,1,0:T(8,128)(2,1)} fusion(bf16[544,3584]{1,0:T(8,128)(2,1)} %get-tuple-element.38, bf16[3584,1176]{1,0:T(8,128)(2,1)} %all-gather.2.cloned.1.call-done), kind=kOutput, calls=%fused_computation.66 | convolution fusion | flops 4586324992 | bytes 13608448 | tf_op jit(solution)/shard_map/dot_general | solution.py:167
  394.0 89.2 %all-reduce.3.cloned.1.call-done = f32[224,1182]{0,1:T(8,128)} async-done(((f32[224,1182]{0,1:T(8,128)}), f32[224,1182]{0,1:T(8,128)}) %all-reduce.3.cloned.1.call-update) | async-done | bytes 1059088 | tf_op jit(solution)/shard_map/psum | solution.py:180
  483.2 1.4 fusion.17
  484.6 1.0 copy.16
  485.7 1.3 fusion.18
  (111 shorter events, 13.7 us)
Async XLA Ops:
  7.2 42.4 %copy-start = (s32[1,272]{1,0:T(1,128)S(1)}, s32[1,272]{1,0:T(1,128)}, u32[]{:S(2)}) copy-start(s32[1,272]{1,0:T(1,128)} %param.9) | copy-start | bytes 3268
  7.2 51.9 %copy-start.6 = (bf16[1,544,1176]{2,1,0:T(8,128)(2,1)S(1)}, bf16[1,544,1176]{2,1,0:T(8,128)(2,1)}, u32[]{:S(2)}) copy-start(bf16[1,544,1176]{2,1,0:T(8,128)(2,1)} %param.7) | copy-start | bytes 3838468
  7.2 57.8 %copy-start.11 = (bf16[5,224]{1,0:T(8,128)(2,1)S(1)}, bf16[5,224]{1,0:T(8,128)(2,1)}, u32[]{:S(2)}) copy-start(bf16[5,224]{1,0:T(8,128)(2,1)} %param.12) | copy-start | bytes 6724
  7.2 121.1 %all-gather.2.cloned.1.call-start = ((), (), s32[]{:S(2)}) async-start(), calls=%async_computation.4 | async-start | bytes 9748480 | tf_op jit(solution)/shard_map/all_gather | solution.py:133
  12.2 52.8 %all-to-all-start = ((bf16[16,2,1]{1,2,0:T(2,128)(2,1)}), bf16[16,2,1]{1,2,0:T(2,128)(2,1)S(1)}, u32[]{:S(2)}, u32[]{:S(2)}) async-start(bf16[16,2,1]{1,2,0:T(2,128)(2,1)} %all_to_all.16), calls=%async_computation | async-start | bytes 16384 | tf_op jit(solution)/shard_map/all_to_all | solution.py:113
  65.6 14.4 %all-to-all-start.2 = ((bf16[16,5,224]{2,1,0:T(8,128)(2,1)}), bf16[16,5,224]{2,1,0:T(8,128)(2,1)S(1)}, u32[]{:S(2)}, u32[]{:S(2)}) async-start(bf16[16,5,224]{2,1,0:T(8,128)(2,1)} %stack.12), calls=%async_computation.2 | async-start | bytes 131072 | tf_op jit(solution)/shard_map/all_to_all | solution.py:124
  80.0 43.8 %all-to-all-start.1 = ((bf16[32,32,1176]{2,1,0:T(8,128)(2,1)}), bf16[32,32,1176]{2,1,0:T(8,128)(2,1)}, u32[]{:S(2)}, u32[]{:S(2)}) async-start(bf16[32,32,1176]{2,1,0:T(8,128)(2,1)} %scatter_fusion), calls=%async_computation.1 | async-start | bytes 5242880 | tf_op jit(solution)/shard_map/all_to_all | solution.py:112
  87.2 293.6 %reduce-scatter.4.cloned.1.call-start = ((), (), s32[]{:S(2)}) async-start(), calls=%async_computation.6 | async-start | bytes 19496960
  136.3 24.1 %copy-start.2 = (f32[544,3584]{1,0:T(8,128)}, f32[544,3584]{1,0:T(8,128)S(1)}, u32[]{:S(2)}) copy-start(f32[544,3584]{1,0:T(8,128)S(1)} %get-tuple-element.65) | copy-start | bytes 23396356
  136.3 15.7 %copy-start.5 = (bf16[1,544,3584]{2,1,0:T(8,128)(2,1)S(1)}, bf16[1,544,3584]{2,1,0:T(8,128)(2,1)}, u32[]{:S(2)}) copy-start(bf16[1,544,3584]{2,1,0:T(8,128)(2,1)} %param.13) | copy-start | bytes 11698180
  136.3 15.7 %copy-start.7 = (f32[17,3584]{1,0:T(8,128)S(1)}, f32[17,3584]{1,0:T(8,128)}, u32[]{:S(2)}) copy-start(f32[17,3584]{1,0:T(8,128)} %get-tuple-element.53) | copy-start | bytes 731140
  136.3 15.7 %copy-start.8 = (f32[17,3584]{1,0:T(8,128)S(1)}, f32[17,3584]{1,0:T(8,128)}, u32[]{:S(2)}) copy-start(f32[17,3584]{1,0:T(8,128)} %get-tuple-element.51) | copy-start | bytes 731140
  136.4 15.7 %copy-start.9 = (f32[17,3584]{1,0:T(8,128)S(1)}, f32[17,3584]{1,0:T(8,128)}, u32[]{:S(2)}) copy-start(f32[17,3584]{1,0:T(8,128)} %get-tuple-element.49) | copy-start | bytes 731140
  136.4 15.7 %copy-start.10 = (f32[17,3584]{1,0:T(8,128)S(1)}, f32[17,3584]{1,0:T(8,128)}, u32[]{:S(2)}) copy-start(f32[17,3584]{1,0:T(8,128)} %get-tuple-element.47) | copy-start | bytes 731140
  137.7 22.7 %copy-start.4 = (bf16[544,3584]{1,0:T(8,128)(2,1)}, bf16[544,3584]{1,0:T(8,128)(2,1)S(1)}, u32[]{:S(2)}) copy-start(bf16[544,3584]{1,0:T(8,128)(2,1)S(1)} %multiply_convert_fusion) | copy-start | bytes 11698180
  137.8 13.0 %collective-permute-start.1 = (bf16[64,3584]{1,0:T(8,128)(2,1)S(1)}, bf16[64,3584]{1,0:T(8,128)(2,1)S(1)}, u32[]{:S(2)}, u32[]{:S(2)}) collective-permute-start(bf16[64,3584]{1,0:T(8,128)(2,1)S(1)} %get-tuple-element.43), channel_id=1, source_target_pairs={{16,0},{32,16},{48,32},{64,48},{80,64},{96,80},{112,96},{128,112},... | collective-permute-start | bytes 1376264 | tf_op jit(solution)/shard_map/ppermute | solution.py:20
  139.3 12.7 %collective-permute-start = (bf16[64,3584]{1,0:T(8,128)(2,1)S(1)}, bf16[64,3584]{1,0:T(8,128)(2,1)S(1)}, u32[]{:S(2)}, u32[]{:S(2)}) collective-permute-start(bf16[64,3584]{1,0:T(8,128)(2,1)S(1)} %get-tuple-element.42), channel_id=1, source_target_pairs={{0,16},{16,32},{32,48},{48,64},{64,80},{80,96},{96,112},{112,128},... | collective-permute-start | bytes 1376264 | tf_op jit(solution)/shard_map/ppermute | solution.py:18
  160.4 1.9 copy-start.3
  163.1 44.3 %collective-permute-start.3 = (bf16[64,3584]{1,0:T(8,128)(2,1)}, bf16[64,3584]{1,0:T(8,128)(2,1)}, u32[]{:S(2)}, u32[]{:S(2)}) collective-permute-start(bf16[64,3584]{1,0:T(8,128)(2,1)} %get-tuple-element.41), channel_id=1, source_target_pairs={{0,16},{16,32},{32,48},{48,64},{64,80},{80,96},{96,112},{112,128},... | collective-permute-start | bytes 1376264 | tf_op jit(solution)/shard_map/ppermute | solution.py:18
  168.4 39.1 %collective-permute-start.2 = (bf16[64,3584]{1,0:T(8,128)(2,1)S(1)}, bf16[64,3584]{1,0:T(8,128)(2,1)}, u32[]{:S(2)}, u32[]{:S(2)}) collective-permute-start(bf16[64,3584]{1,0:T(8,128)(2,1)S(1)} %get-tuple-element.40), channel_id=1, source_target_pairs={{16,0},{32,16},{48,32},{64,48},{80,64},{96,80},{112,96},{128,112},... | collective-permute-start | bytes 1376264 | tf_op jit(solution)/shard_map/ppermute | solution.py:20
  207.3 10.4 %slice-start = ((s8[7798784]{0:T(1024)(128)(4,1)}), s8[4194304]{0:T(1024)(128)(4,1)S(1)}, s32[]{:S(2)}) async-start(s8[7798784]{0:T(1024)(128)(4,1)} %bitcast.109), calls=%async_computation.7 | async-start | bytes 8388608
  207.5 10.3 %slice-start.1 = ((s8[7798784]{0:T(1024)(128)(4,1)}), s8[3604480]{0:T(1024)(128)(4,1)S(1)}, s32[]{:S(2)}) async-start(s8[7798784]{0:T(1024)(128)(4,1)} %bitcast.109), calls=%async_computation.8 | async-start | bytes 7208960
  272.9 210.3 %all-reduce.3.cloned.1.call-start = ((), (), s32[]{:S(2)}) async-start(), calls=%async_computation.5 | async-start | bytes 2424832 | tf_op jit(solution)/shard_map/psum | solution.py:180
  383.5 103.4 %copy-start.1 = (s32[1,272]{1,0:T(1,128)S(1)}, s32[1,272]{1,0:T(1,128)}, u32[]{:S(2)}) copy-start(s32[1,272]{1,0:T(1,128)} %param.9) | copy-start | bytes 3268
Sparse Core Ops, SparseCore 0:
  9.9 60.9 all-gather.1
  273.0 107.7 reduce-scatter.3
  384.1 99.0 all-reduce.2
